TPU v7x, 32 devices: a whole 2x2x4 slice. The times are simulated.
32 devices in a mesh: row: 8 (over z, x), col: 4 (over y, core).
Axes of the slice: x: 2, y: 2, z: 4, core: 2. Of those that a mesh axis runs over, the one named last changes fastest.
Arguments:
- points: bfloat16 [48, 1024, 1024], P('row', 'col')
- targets: bfloat16 [48, 1024, 1000], P('row', 'col'), may hold values from -6 to 6
- coeffs: float32 [48, 1024, 1000], P('row', 'col'), may hold values from -0.375 to 0.375
- block_inverse: float32 [48, 1024, 1024], P('row', 'col')
- block_order: int32 [48], replicated, may hold values from 0 to 47, each once
Outputs:
- coeffs_out: float32 [48, 1024, 1000], P('row', 'col')
All inputs are finite; a program needn't handle non-finite values.
Results may differ from a plain program's by a relative error of at most 0.0003.
Values may be sent and summed in bfloat16 or wider, within the bound.
No kernel may reach another device: no remote copies, remote signals or barrier semaphores. Data moves between devices by JAX's collectives and lax.ppermute only.
A program may use at most 128 MiB of HBM per device.

v0:
```python
import jax
import jax.numpy as jnp
from jax import lax
from jax.sharding import PartitionSpec as P

STEPS = 2
ridge_weight = 1.0


def broadcast(value, axis, source):
    kept = jnp.where(lax.axis_index(axis) == source, value, 0).astype(value.dtype)
    return lax.psum(kept, axis)


def on_device(points, targets, coeffs, block_inverse, block_order):
    blocks_here, per_col, features = points.shape
    classes = targets.shape[2]
    my_row = lax.axis_index("row")
    my_col = lax.axis_index("col")
    flat_points = points.reshape(blocks_here * per_col, features)
    flat_wide = flat_points.astype(jnp.float32)
    point_squares = jnp.sum(flat_wide * flat_wide, axis=1)
    current = coeffs
    for sweep_step in range(STEPS):
        block_id = block_order[sweep_step]
        local_index = block_id % blocks_here
        owner_row = block_id // blocks_here
        own_slice = lax.dynamic_index_in_dim(points, local_index, 0, keepdims=False)
        slice_part = broadcast(own_slice, "row", owner_row)
        active = lax.all_gather(slice_part, "col", axis=0, tiled=True)
        active_wide = active.astype(jnp.float32)
        active_squares = jnp.sum(active_wide * active_wide, axis=1)
        inner = lax.dot_general(
            active, flat_points, (((1,), (1,)), ((), ())), preferred_element_type=jnp.float32
        )
        distance = active_squares[:, None] + point_squares[None, :] - 2.0 * inner
        tile_wide = jnp.exp(-distance * (0.5 / features))
        flat_current = current.reshape(blocks_here * per_col, classes)
        products = jnp.dot(
            tile_wide,
            flat_current,
            precision=lax.Precision.HIGHEST,
            preferred_element_type=jnp.float32,
        )
        summed = lax.psum(products, ("row", "col"))
        own_sum = lax.dynamic_slice_in_dim(summed, my_col * per_col, per_col, 0)
        previous = lax.dynamic_index_in_dim(current, local_index, 0, keepdims=False)
        wanted = lax.dynamic_index_in_dim(targets, local_index, 0, keepdims=False).astype(
            jnp.float32
        )
        residual = wanted - own_sum - ridge_weight * previous
        full_residual = lax.all_gather(residual, "col", axis=0, tiled=True)
        inverse_rows = lax.dynamic_index_in_dim(block_inverse, local_index, 0, keepdims=False)
        increment = jnp.dot(
            inverse_rows,
            full_residual,
            precision=lax.Precision.HIGHEST,
            preferred_element_type=jnp.float32,
        )
        updated = jnp.where(my_row == owner_row, previous + increment, previous)
        current = lax.dynamic_update_index_in_dim(current, updated, local_index, 0)
    return current


def solution(mesh):
    placed = (
        P("row", "col", None),
        P("row", "col", None),
        P("row", "col", None),
        P("row", "col", None),
        P(),
    )
    return jax.shard_map(
        on_device, mesh=mesh, in_specs=placed, out_specs=P("row", "col", None), check_vma=False
    )
```

profile of v0, /device:TPU:0, one launch (start us, length us, event | category | flops | bytes accessed | tf_op | source)
XLA Modules:
  0.0 587.3 jit_solution(10391976789681587924)
XLA Ops:
  6.5 6.0 %copy.15 = f32[6,256,1000]{1,2,0:T(8,128)} copy(f32[6,256,1000]{1,2,0:T(8,128)} %param.7) | data formatting | bytes 12288000
  16.7 1.1 select_bitcast_fusion
  17.8 81.1 %all-reduce.9.cloned.1.call-done = (bf16[256,1024]{1,0:T(8,128)(2,1)}, bf16[256,1024]{1,0:T(8,128)(2,1)}) async-done(((bf16[256,1024]{1,0:T(8,128)(2,1)}, bf16[256,1024]{1,0:T(8,128)(2,1)}), (bf16[256,1024]{1,0:T(8,128)(2,1)}, bf16[256,1024]{1,0:T(8,128)(2,1)})) %all-reduce.9.cloned.1.call-update) | async-done | bytes 1048592 | tf_op jit(solution)/shard_map/psum | solution.py:12
  99.0 6.5 %copy.6 = f32[6,256,1000]{2,1,0:T(8,128)} copy(f32[6,256,1000]{1,2,0:T(8,128)} %copy.15) | data formatting | bytes 12288000 | tf_op args[2]
  105.5 0.7 multiply_reduce_fusion
  106.2 16.5 %all-gather.5.cloned.1.call-done = bf16[1024,1024]{1,0:T(8,128)(2,1)} async-done(((bf16[256,1024]{1,0:T(8,128)(2,1)}), bf16[1024,1024]{1,0:T(8,128)(2,1)}) %all-gather.5.cloned.1.call-update) | async-done | bytes 2097168 | tf_op jit(solution)/shard_map/all_gather | solution.py:30
  122.7 2.2 multiply_reduce_fusion.2
  124.9 5.2 fusion.39
  130.2 23.8 %fusion.7 = f32[1024,1000]{0,1:T(8,128)} fusion(f32[1536,1000]{1,0:T(8,128)S(1)} %bitcast.49, f32[1024,1536]{1,0:T(8,128)S(1)} %fusion.39, f32[1536]{0:T(1024)S(1)} %add.75, f32[1024]{0:T(1024)S(1)} %multiply_reduce_fusion.2), kind=kOutput, calls=%fused_computation.7 | convolution fusion | flops 18882232320 | bytes 16541696 | tf_op jit(solution)/shard_map/dot_general | solution.py:39
  154.6 141.3 %all-reduce.5.cloned.1.call-done = f32[1024,1000]{0,1:T(8,128)} async-done(((f32[1024,1000]{0,1:T(8,128)}), f32[1024,1000]{0,1:T(8,128)}) %all-reduce.5.cloned.1.call-update) | async-done | bytes 4096016 | tf_op jit(solution)/shard_map/psum | solution.py:45
  295.9 2.9 fusion.31
  298.9 2.3 constant_dynamic-slice_fusion.1
  301.1 18.6 %all-gather.9.cloned.1.call-done = bf16[1024,1024]{1,0:T(8,128)(2,1)} async-done(((bf16[256,1024]{1,0:T(8,128)(2,1)}), bf16[1024,1024]{1,0:T(8,128)(2,1)}) %all-gather.9.cloned.1.call-update) | async-done | bytes 2097168 | tf_op jit(solution)/shard_map/all_gather | solution.py:30
  319.7 2.1 multiply_reduce_fusion.1
  321.8 18.4 %fusion.40 = f32[1024,1536]{1,0:T(8,128)} fusion(bf16[1024,1024]{1,0:T(8,128)(2,1)} %all-gather.9.cloned.1.call-done, bf16[1536,1024]{1,0:T(8,128)(2,1)S(1)} %bitcast.52), kind=kOutput, calls=%fused_computation.51 | convolution fusion | flops 3221225472 | bytes 11534336 | tf_op jit(solution)/shard_map/dot_general | solution.py:33
  340.2 14.8 %all-gather.7.cloned.1.call-done = f32[1024,1000]{0,1:T(8,128)} async-done(((f32[256,1000]{0,1:T(8,128)}), f32[1024,1000]{0,1:T(8,128)}) %all-gather.7.cloned.1.call-update) | async-done | bytes 4096016 | tf_op jit(solution)/shard_map/all_gather | solution.py:52
  355.1 7.1 %fusion.25 = f32[6,256,1000]{1,2,0:T(8,128)} fusion(f32[6,256,1000]{1,2,0:T(8,128)} %copy.15, s32[]{:T(128)S(6)} %select_n.78, f32[1024,1000]{0,1:T(8,128)} %all-gather.7.cloned.1.call-done, f32[6,256,1024]{2,1,0:T(8,128)} %param.8, f32[1,256,1000]{1,2,0:T(8,128)} %constant_dynamic-slice_fusion.1, pred[]{:T(512)S(6)} %eq.11), kind=kOutput, calls=%fused_computation.30 | convolution fusion | flops 3146240000 | bytes 7194112 | tf_op jit(solution)/shard_map/dot_general | solution.py:54
  362.2 6.5 %copy.7 = f32[6,256,1000]{2,1,0:T(8,128)} copy(f32[6,256,1000]{1,2,0:T(8,128)} %fusion.25) | data formatting | bytes 12288000 | tf_op jit(solution)/shard_map/jit(dynamic_update_index_in_dim)/dynamic_update_slice | solution.py:61
  368.7 26.1 %fusion = f32[1024,1000]{0,1:T(8,128)} fusion(f32[1536,1000]{1,0:T(8,128)} %bitcast.50, f32[1024,1536]{1,0:T(8,128)} %fusion.40, f32[1024]{0:T(1024)S(1)} %multiply_reduce_fusion.1, f32[1536]{0:T(1024)S(1)} %add.75), kind=kOutput, calls=%fused_computation | convolution fusion | flops 18882232320 | bytes 16541696 | tf_op jit(solution)/shard_map/dot_general | solution.py:39
  395.1 141.7 %all-reduce.7.cloned.1.call-done = f32[1024,1000]{0,1:T(8,128)} async-done(((f32[1024,1000]{0,1:T(8,128)}), f32[1024,1000]{0,1:T(8,128)}) %all-reduce.7.cloned.1.call-update) | async-done | bytes 4096016 | tf_op jit(solution)/shard_map/psum | solution.py:45
  536.8 2.8 fusion.30
  539.6 1.3 constant_dynamic-slice_fusion
  540.9 32.5 %all-gather.11.cloned.1.call-done = f32[1024,1000]{0,1:T(8,128)} async-done(((f32[256,1000]{0,1:T(8,128)}), f32[1024,1000]{0,1:T(8,128)}) %all-gather.11.cloned.1.call-update) | async-done | bytes 4096016 | tf_op jit(solution)/shard_map/all_gather | solution.py:52
  573.4 6.8 %fusion.23 = f32[6,256,1000]{1,2,0:T(8,128)} fusion(f32[6,256,1000]{1,2,0:T(8,128)} %fusion.25, s32[]{:T(128)S(6)} %select_n.87, f32[1024,1000]{0,1:T(8,128)} %all-gather.11.cloned.1.call-done, f32[6,256,1024]{2,1,0:T(8,128)} %param.8, f32[1,256,1000]{1,2,0:T(8,128)S(1)} %constant_dynamic-slice_fusion, pred[]{:T(512)S(6)} %eq.12), kind=kOutput, calls=%fused_computation.28 | convolution fusion | flops 3146240000 | bytes 7194112 | tf_op jit(solution)/shard_map/dot_general | solution.py:54
  (25 shorter events, 1.7 us)
Async XLA Ops:
  6.5 10.2 %copy-start = (bf16[6,256,1024]{2,1,0:T(8,128)(2,1)S(1)}, bf16[6,256,1024]{2,1,0:T(8,128)(2,1)}, u32[]{:S(2)}) copy-start(bf16[6,256,1024]{2,1,0:T(8,128)(2,1)} %param.5) | copy-start | bytes 9437188
  6.5 6.0 %copy-start.1 = (s32[48]{0:T(128)S(1)}, s32[48]{0:T(128)}, u32[]{:S(2)}) copy-start(s32[48]{0:T(128)} %param.9) | copy-start | bytes 580
  6.5 92.4 %all-reduce.9.cloned.1.call-start = ((), (), s32[]{:S(2)}) async-start(), calls=%async_computation.6 | async-start | bytes 2097152 | tf_op jit(solution)/shard_map/psum | solution.py:12
  17.8 104.9 %all-gather.5.cloned.1.call-start = ((), (), s32[]{:S(2)}) async-start(), calls=%async_computation | async-start | bytes 2621440 | tf_op jit(solution)/shard_map/all_gather | solution.py:30
  98.9 197.0 %all-reduce.5.cloned.1.call-start = ((), (), s32[]{:S(2)}) async-start(), calls=%async_computation.1 | async-start | bytes 8192000 | tf_op jit(solution)/shard_map/psum | solution.py:45
  122.7 7.4 %slice-start = ((s8[6291456]{0:T(1024)(128)(4,1)}), s8[4194304]{0:T(1024)(128)(4,1)S(1)}, s32[]{:S(2)}) async-start(s8[6291456]{0:T(1024)(128)(4,1)} %bitcast.47), calls=%async_computation.7 | async-start | bytes 8388608
  124.9 5.2 slice-start.1
  154.0 165.7 %all-gather.9.cloned.1.call-start = ((), (), s32[]{:S(2)}) async-start(), calls=%async_computation.3 | async-start | bytes 2621440 | tf_op jit(solution)/shard_map/all_gather | solution.py:30
  154.6 200.5 %all-gather.7.cloned.1.call-start = ((), (), s32[]{:S(2)}) async-start(), calls=%async_computation.2 | async-start | bytes 5120000 | tf_op jit(solution)/shard_map/all_gather | solution.py:52
  298.8 237.9 %all-reduce.7.cloned.1.call-start = ((), (), s32[]{:S(2)}) async-start(), calls=%async_computation.4 | async-start | bytes 8192000 | tf_op jit(solution)/shard_map/psum | solution.py:45
  394.8 178.6 %all-gather.11.cloned.1.call-start = ((), (), s32[]{:S(2)}) async-start(), calls=%async_computation.5 | async-start | bytes 5120000 | tf_op jit(solution)/shard_map/all_gather | solution.py:52
Sparse Core Ops, SparseCore 0:
  17.9 80.9 all-reduce.8
  100.5 22.1 all-gather.4
  154.1 141.7 all-reduce.4
  297.4 22.3 all-gather.8
  321.1 33.8 all-gather.6
  395.0 141.7 all-reduce.6
  539.7 33.6 all-gather.10
where the time goes:
time: 592 us; the launch traced here: 587 us
  waiting for transfers between devices  447 us (76%)
  matrix products  87.5 us (15%)
  local copies, waits for them, and re-layouts  23.2 us (4%)
  between operations  17.4 us (3%)
  other arithmetic  11.7 us (2%)
    psum x2, waiting for transfers between devices, on_device(): summed = lax.psum(products, ('row', 'col'))  283 us
    psum x1, waiting for transfers between devices, broadcast(): return lax.psum(kept, axis)  81.1 us
    dot_general x2, matrix products, on_device(): jnp.dot(tile_wide, flat_current, precision=lax.Precision.HIGHEST, preferr...  49.9 us
    all_gather x2, waiting for transfers between devices, on_device(): full_residual = lax.all_gather(residual, 'col', axis=0, tiled=True)  47.3 us
    all_gather x2, waiting for transfers between devices, on_device(): active = lax.all_gather(slice_part, 'col', axis=0, tiled=True)  35.1 us
    dot_general x2, matrix products, on_device(): lax.dot_general(active, flat_points, (((1,), (1,)), ((), ())), preferred_...  23.6 us
    dot_general x2, matrix products, on_device(): jnp.dot(inverse_rows, full_residual, precision=lax.Precision.HIGHEST, pre...  13.9 us
    unnamed x10, local copies, waits for them, and re-layouts  12.5 us
  transfers between devices with their start and end apart: 7, of which 7 were waited for; matrix products, arithmetic and copies ran while one was open for 6% of the time, Pallas kernels for 0%

commit v1 on v0

--- a/solution.py
+++ b/solution.py
@@ -42,7 +42,9 @@
             precision=lax.Precision.HIGHEST,
             preferred_element_type=jnp.float32,
         )
-        summed = lax.psum(products, ("row", "col"))
+        summed = products
+        for name in ("col", "row"):
+            summed = lax.psum(summed, name)
         own_sum = lax.dynamic_slice_in_dim(summed, my_col * per_col, per_col, 0)
         previous = lax.dynamic_index_in_dim(current, local_index, 0, keepdims=False)
         wanted = lax.dynamic_index_in_dim(targets, local_index, 0, keepdims=False).astype(

time: 592 us -> 790 us (1.33)
  waiting for transfers between devices: 447 us -> 645 us
    psum x2 -> x4, waiting for transfers between devices: 283 us -> 482 us  [on_device(): summed = lax.psum(summed, name)]
  transfers between devices with their start and end apart: 7 -> 9, of which waited for: 7 -> 9; matrix products, arithmetic and copies ran while one was open for 6% -> 4% of each run, Pallas kernels for 0% -> 0%
where the time goes in v1:
time: 790 us; the launch traced here: 785 us
  waiting for transfers between devices  645 us (82%)
  matrix products  87.5 us (11%)
  local copies, waits for them, and re-layouts  23.2 us (3%)
  between operations  17.1 us (2%)
  other arithmetic  11.7 us (1%)
    psum x4, waiting for transfers between devices, on_device(): summed = lax.psum(summed, name)  482 us
    psum x1, waiting for transfers between devices, broadcast(): return lax.psum(kept, axis)  81.1 us
    dot_general x2, matrix products, on_device(): jnp.dot(tile_wide, flat_current, precision=lax.Precision.HIGHEST, preferr...  49.9 us
    all_gather x2, waiting for transfers between devices, on_device(): full_residual = lax.all_gather(residual, 'col', axis=0, tiled=True)  46.6 us
    all_gather x2, waiting for transfers between devices, on_device(): active = lax.all_gather(slice_part, 'col', axis=0, tiled=True)  34.3 us
    dot_general x2, matrix products, on_device(): lax.dot_general(active, flat_points, (((1,), (1,)), ((), ())), preferred_...  23.7 us
  transfers between devices with their start and end apart: 9, of which 9 were waited for; matrix products, arithmetic and copies ran while one was open for 4% of the time, Pallas kernels for 0%

profile of v1, /device:TPU:0, one launch (start us, length us, event | category | flops | bytes accessed | tf_op | source)
XLA Modules:
  0.0 785.0 jit_solution(9437434270645593975)
XLA Ops:
  6.5 6.0 copy.17
  17.8 81.1 %all-reduce.15.cloned.1.call-done = (bf16[256,1024]{1,0:T(8,128)(2,1)}, bf16[256,1024]{1,0:T(8,128)(2,1)}) async-done(((bf16[256,1024]{1,0:T(8,128)(2,1)}, bf16[256,1024]{1,0:T(8,128)(2,1)}), (bf16[256,1024]{1,0:T(8,128)(2,1)}, bf16[256,1024]{1,0:T(8,128)(2,1)})) %all-reduce.15.cloned.1.call-update) | async-done | bytes 1048592 | tf_op jit(solution)/shard_map/psum | solution.py:12
  99.0 6.5 copy.6
  106.2 16.5 %all-gather.5.cloned.1.call-done = bf16[1024,1024]{1,0:T(8,128)(2,1)} async-done(((bf16[256,1024]{1,0:T(8,128)(2,1)}), bf16[1024,1024]{1,0:T(8,128)(2,1)}) %all-gather.5.cloned.1.call-update) | async-done | bytes 2097168 | tf_op jit(solution)/shard_map/all_gather | solution.py:30
  122.7 2.2 multiply_reduce_fusion.2
  124.9 5.2 fusion.39
  130.2 23.8 %fusion.7 = f32[1024,1000]{0,1:T(8,128)} fusion(f32[1536,1000]{1,0:T(8,128)S(1)} %bitcast.49, f32[1024,1536]{1,0:T(8,128)S(1)} %fusion.39, f32[1536]{0:T(1024)S(1)} %add.79, f32[1024]{0:T(1024)S(1)} %multiply_reduce_fusion.2), kind=kOutput, calls=%fused_computation.7 | convolution fusion | flops 18882232320 | bytes 16541696 | tf_op jit(solution)/shard_map/dot_general | solution.py:39
  154.0 84.0 %all-reduce.7.cloned.1.call-done = f32[1024,1000]{0,1:T(8,128)} async-done(((f32[1024,1000]{0,1:T(8,128)}), f32[1024,1000]{0,1:T(8,128)}) %all-reduce.7.cloned.1.call-update) | async-done | bytes 4096016 | tf_op jit(solution)/shard_map/psum | solution.py:47
  238.7 156.9 %all-reduce.9.cloned.1.call-done = f32[1024,1000]{0,1:T(8,128)} async-done(((f32[1024,1000]{0,1:T(8,128)}), f32[1024,1000]{0,1:T(8,128)}) %all-reduce.9.cloned.1.call-update) | async-done | bytes 4096016 | tf_op jit(solution)/shard_map/psum | solution.py:47
  395.6 2.9 fusion.31
  398.5 2.3 constant_dynamic-slice_fusion.1
  400.8 17.8 %all-gather.9.cloned.1.call-done = bf16[1024,1024]{1,0:T(8,128)(2,1)} async-done(((bf16[256,1024]{1,0:T(8,128)(2,1)}), bf16[1024,1024]{1,0:T(8,128)(2,1)}) %all-gather.9.cloned.1.call-update) | async-done | bytes 2097168 | tf_op jit(solution)/shard_map/all_gather | solution.py:30
  418.6 2.1 multiply_reduce_fusion.1
  420.7 18.5 %fusion.40 = f32[1024,1536]{1,0:T(8,128)} fusion(bf16[1024,1024]{1,0:T(8,128)(2,1)} %all-gather.9.cloned.1.call-done, bf16[1536,1024]{1,0:T(8,128)(2,1)S(1)} %bitcast.52), kind=kOutput, calls=%fused_computation.51 | convolution fusion | flops 3221225472 | bytes 11534336 | tf_op jit(solution)/shard_map/dot_general | solution.py:33
  439.1 14.8 %all-gather.7.cloned.1.call-done = f32[1024,1000]{0,1:T(8,128)} async-done(((f32[256,1000]{0,1:T(8,128)}), f32[1024,1000]{0,1:T(8,128)}) %all-gather.7.cloned.1.call-update) | async-done | bytes 4096016 | tf_op jit(solution)/shard_map/all_gather | solution.py:54
  453.9 7.1 fusion.25
  461.0 6.5 copy.7
  467.5 26.1 %fusion = f32[1024,1000]{0,1:T(8,128)} fusion(f32[1536,1000]{1,0:T(8,128)} %bitcast.50, f32[1024,1536]{1,0:T(8,128)} %fusion.40, f32[1024]{0:T(1024)S(1)} %multiply_reduce_fusion.1, f32[1536]{0:T(1024)S(1)} %add.79), kind=kOutput, calls=%fused_computation | convolution fusion | flops 18882232320 | bytes 16541696 | tf_op jit(solution)/shard_map/dot_general | solution.py:39
  493.8 84.0 %all-reduce.11.cloned.1.call-done = f32[1024,1000]{0,1:T(8,128)} async-done(((f32[1024,1000]{0,1:T(8,128)}), f32[1024,1000]{0,1:T(8,128)}) %all-reduce.11.cloned.1.call-update) | async-done | bytes 4096016 | tf_op jit(solution)/shard_map/psum | solution.py:47
  578.0 157.4 %all-reduce.13.cloned.1.call-done = f32[1024,1000]{0,1:T(8,128)} async-done(((f32[1024,1000]{0,1:T(8,128)}), f32[1024,1000]{0,1:T(8,128)}) %all-reduce.13.cloned.1.call-update) | async-done | bytes 4096016 | tf_op jit(solution)/shard_map/psum | solution.py:47
  735.5 2.9 fusion.30
  738.4 1.3 constant_dynamic-slice_fusion
  739.7 31.8 %all-gather.11.cloned.1.call-done = f32[1024,1000]{0,1:T(8,128)} async-done(((f32[256,1000]{0,1:T(8,128)}), f32[1024,1000]{0,1:T(8,128)}) %all-gather.11.cloned.1.call-update) | async-done | bytes 4096016 | tf_op jit(solution)/shard_map/all_gather | solution.py:54
  771.4 6.8 fusion.23
  (31 shorter events, 3.5 us)
Async XLA Ops:
  6.5 10.2 %copy-start = (bf16[6,256,1024]{2,1,0:T(8,128)(2,1)S(1)}, bf16[6,256,1024]{2,1,0:T(8,128)(2,1)}, u32[]{:S(2)}) copy-start(bf16[6,256,1024]{2,1,0:T(8,128)(2,1)} %param.5) | copy-start | bytes 9437188
  6.5 6.0 copy-start.1
  6.5 92.4 %all-reduce.15.cloned.1.call-start = ((), (), s32[]{:S(2)}) async-start(), calls=%async_computation.8 | async-start | bytes 2097152 | tf_op jit(solution)/shard_map/psum | solution.py:12
  17.8 104.9 %all-gather.5.cloned.1.call-start = ((), (), s32[]{:S(2)}) async-start(), calls=%async_computation | async-start | bytes 2621440 | tf_op jit(solution)/shard_map/all_gather | solution.py:30
  98.9 139.1 %all-reduce.7.cloned.1.call-start = ((), (), s32[]{:S(2)}) async-start(), calls=%async_computation.1 | async-start | bytes 8192000 | tf_op jit(solution)/shard_map/psum | solution.py:47
  122.7 7.4 slice-start
  124.9 5.2 slice-start.1
  154.0 241.6 %all-reduce.9.cloned.1.call-start = ((), (), s32[]{:S(2)}) async-start(), calls=%async_computation.2 | async-start | bytes 8192000 | tf_op jit(solution)/shard_map/psum | solution.py:47
  238.1 180.5 %all-gather.9.cloned.1.call-start = ((), (), s32[]{:S(2)}) async-start(), calls=%async_computation.4 | async-start | bytes 2621440 | tf_op jit(solution)/shard_map/all_gather | solution.py:30
  238.7 215.3 %all-gather.7.cloned.1.call-start = ((), (), s32[]{:S(2)}) async-start(), calls=%async_computation.3 | async-start | bytes 5120000 | tf_op jit(solution)/shard_map/all_gather | solution.py:54
  398.5 179.3 %all-reduce.11.cloned.1.call-start = ((), (), s32[]{:S(2)}) async-start(), calls=%async_computation.5 | async-start | bytes 8192000 | tf_op jit(solution)/shard_map/psum | solution.py:47
  493.7 241.7 %all-reduce.13.cloned.1.call-start = ((), (), s32[]{:S(2)}) async-start(), calls=%async_computation.6 | async-start | bytes 8192000 | tf_op jit(solution)/shard_map/psum | solution.py:47
  577.8 193.6 %all-gather.11.cloned.1.call-start = ((), (), s32[]{:S(2)}) async-start(), calls=%async_computation.7 | async-start | bytes 5120000 | tf_op jit(solution)/shard_map/all_gather | solution.py:54
Sparse Core Ops, SparseCore 0:
  17.9 80.9 all-reduce.14
  100.5 22.1 all-gather.4
  154.1 83.8 all-reduce.6
  241.6 153.9 all-reduce.8
  397.0 21.5 all-gather.8
  420.0 33.8 all-gather.6
  493.8 83.8 all-reduce.10
  581.4 153.9 all-reduce.12
  738.5 32.9 all-gather.10
